TPU v7x, 256 devices: a whole 4x4x8 slice. The times are simulated.
256 devices in a mesh: dp: 32 (over x, z_hi, y), col: 8 (over z_lo, core).
Axes of the slice: x: 4, y: 4, z: 8 (z_hi: 2, z_lo: 4; z = z_hi * 4 + z_lo), core: 2. Of those that a mesh axis runs over, the one named last changes fastest.
Arguments:
- embeddings: bfloat16 [16384, 4096], P('dp'), may hold values from -16 to 16
- rotation: bfloat16 [4096, 4096], P(None, 'col'), may hold values from -0.09375 to 0.09375
- codes: int32 [16384, 512], P('dp', 'col'), may hold values from 0 to 255
- codebooks: bfloat16 [512, 256, 8], P('col'), may hold values from -16 to 16
Outputs:
- new_rotation: float32 [4096, 4096], P('dp', 'col')
All inputs are finite; a program needn't handle non-finite values.
Results may differ from a plain program's by a relative error of at most 0.015.
Values may be sent and summed in bfloat16 or wider, within the bound.
A program may use at most 64 MiB of HBM per device.

v0:
```python
import math
import jax
import jax.numpy as jnp
from jax import lax
from jax.sharding import PartitionSpec as P

STEPS = 2


def rebuild_rows(codes, codebooks):
    tok_rows, sub_count = codes.shape
    centroids = codebooks.shape[1]
    sub_width = codebooks.shape[2]
    group_size = min(16, sub_count)
    centroid_ids = jnp.arange(centroids, dtype=jnp.int32)
    diag_eye = jnp.eye(group_size, dtype=jnp.bfloat16)
    pieces = []
    for first_sub in range(0, sub_count, group_size):
        sub_ids = codes[:, first_sub : first_sub + group_size]
        onehot = (sub_ids[:, :, None] == centroid_ids[None, None, :]).astype(jnp.bfloat16)
        onehot = onehot.reshape(tok_rows, group_size * centroids)
        block_table = (
            codebooks[first_sub : first_sub + group_size][:, :, None, :]
            * diag_eye[:, None, :, None]
        )
        block_table = block_table.reshape(group_size * centroids, group_size * sub_width)
        pieces.append(
            jnp.dot(onehot, block_table, preferred_element_type=jnp.float32).astype(jnp.bfloat16)
        )
    return jnp.concatenate(pieces, axis=1)


def contract_rows(left_rows, right_rows):
    return lax.dot_general(
        left_rows, right_rows, (((0,), (0,)), ((), ())), preferred_element_type=jnp.float32
    )


def shards(embeddings, rotation, codes, codebooks):
    tok_rows, model_width = embeddings.shape
    rows_total = tok_rows * lax.axis_size("dp")
    block_rows = model_width // lax.axis_size("dp")
    rotated = jnp.dot(embeddings, rotation, preferred_element_type=jnp.float32)
    rebuilt = rebuild_rows(codes, codebooks)
    rebuilt_wide = rebuilt.astype(jnp.float32)
    residue = rotated - rebuilt_wide
    partial_value = jnp.sum(residue * residue, axis=1)
    row_error = lax.psum(partial_value, "col")
    weights = 1.0 / (1.0 + row_error / (2.0 * model_width))
    weighted = (weights[:, None] * rebuilt_wide).astype(jnp.bfloat16)
    cross_block = lax.psum_scatter(
        contract_rows(embeddings, weighted), "dp", scatter_dimension=0, tiled=True
    )
    start_row = lax.axis_index("dp") * block_rows
    prior_block = lax.dynamic_slice_in_dim(rotation, start_row, block_rows, 0).astype(jnp.float32)
    cross_block = cross_block + 0.2 * rows_total * prior_block
    frob_total = lax.psum(jnp.sum(cross_block * cross_block), ("dp", "col"))
    norm_scale = 1.4 * jnp.sqrt(frob_total / model_width)
    iterate = cross_block / norm_scale
    for step_index in range(STEPS):
        half_iter = iterate.astype(jnp.bfloat16)
        row_panel = lax.all_gather(half_iter, "col", axis=1, tiled=True)
        gram_block = lax.psum_scatter(
            contract_rows(row_panel, half_iter).astype(jnp.bfloat16),
            "dp",
            scatter_dimension=0,
            tiled=True,
        )
        product = jnp.dot(
            row_panel,
            lax.all_gather(gram_block, "dp", axis=0, tiled=True),
            preferred_element_type=jnp.float32,
        )
        iterate = 1.5 * iterate - 0.5 * product
    return math.sqrt(model_width) * iterate


def solution(mesh):
    placed = (P("dp", None), P(None, "col"), P("dp", "col"), P("col", None, None))
    return jax.shard_map(
        shards, mesh=mesh, in_specs=placed, out_specs=P("dp", "col"), check_vma=False
    )
```

profile of v0, /device:TPU:32, one launch (start us, length us, event | category | flops | bytes accessed | tf_op | source)
XLA Modules:
  0.0 1196.8 jit_solution(9498834475879376770)
XLA Ops:
  6.5 1.0 fusion.12
  7.6 0.4 multiply_bitcast_fusion.3
  8.0 1.4 copy.37
  9.4 0.1 copy.21
  9.6 3.0 iota_compare_fusion.1
  12.6 2.9 copy.36
  15.5 1.5 copy.35
  17.0 0.1 copy.19
  17.1 3.0 iota_compare_fusion.2
  20.1 2.9 copy.34
  23.0 1.5 copy.33
  24.5 0.1 copy.17
  24.6 3.0 iota_compare_fusion.3
  27.6 3.0 copy.32
  30.6 1.4 copy.39
  32.0 0.1 copy.23
  32.1 3.2 iota_compare_fusion
  35.3 1.6 copy.38
  36.9 2.9 convolution_convert_fusion.3
  39.9 1.5 convolution_convert_fusion.4
  41.4 0.0 copy-done.5
  41.4 0.3 copy-done.8
  41.7 1.5 convolution_convert_fusion.5
  43.3 1.5 convolution_convert_fusion.2
  44.8 0.6 copy-done.1
  45.4 1.3 copy-done.11
  46.7 2.4 fusion.1
  49.1 13.7 %psum.14 = f32[512]{0:T(512)S(1)} all-reduce(f32[512]{0:T(512)S(1)} %fusion.1), channel_id=1, replica_groups=mesh['dp'=32,'col'=8] {'col'}, use_global_device_ids=true, to_apply=%region_1.0 | all-reduce | flops 512 | bytes 4096 | tf_op jit(solution)/shard_map/psum | solution.py:48
  62.8 7.8 convolution_bitcast_fusion
  70.7 0.9 constant_dynamic-slice_fusion
  71.6 0.1 copy.31
  71.7 268.2 %reduce-scatter.4.cloned.1.call-done = f32[128,512]{0,1:T(8,128)} async-done(((f32[4096,512]{0,1:T(8,128)}), f32[128,512]{0,1:T(8,128)}) %reduce-scatter.4.cloned.1.call-update) | async-done | bytes 262160 | tf_op jit(solution)/shard_map/reduce_scatter | solution.py:51
  339.9 1.6 multiply_reduce_fusion
  341.5 73.1 %psum.15 = f32[]{:T(128)} all-reduce(f32[]{:T(128)} %multiply_reduce_fusion), channel_id=1, replica_groups=mesh['dp'=32,'col'=8] {'dp','col'}, use_global_device_ids=true, to_apply=%region_4.0 | all-reduce | flops 1 | bytes 8 | tf_op jit(solution)/shard_map/psum | solution.py:57
  415.3 1.7 fusion.9
  417.0 0.3 reduce-scatter.6.cloned.1.call-start
  417.2 30.9 %all-gather.5.cloned.1.call-done = bf16[128,4096]{0,1:T(8,128)(2,1)} async-done(((bf16[128,512]{0,1:T(8,128)(2,1)}), bf16[128,4096]{0,1:T(8,128)(2,1)}) %all-gather.5.cloned.1.call-update) | async-done | bytes 1048592 | tf_op jit(solution)/shard_map/all_gather | solution.py:62
  448.1 4.4 convolution_convert_fusion.1
  452.7 240.5 %reduce-scatter.6.cloned.1.call-done = bf16[128,512]{1,0:T(8,128)(2,1)} async-done(((bf16[4096,512]{1,0:T(8,128)(2,1)}), bf16[128,512]{1,0:T(8,128)(2,1)}) %reduce-scatter.6.cloned.1.call-update) | async-done | bytes 131088 | tf_op jit(solution)/shard_map/reduce_scatter | solution.py:63
  693.2 106.7 %all-gather.7.cloned.1.call-done = bf16[4096,512]{1,0:T(8,128)(2,1)} async-done(((bf16[128,512]{1,0:T(8,128)(2,1)}), bf16[4096,512]{1,0:T(8,128)(2,1)}) %all-gather.7.cloned.1.call-update) | async-done | bytes 4194320 | tf_op jit(solution)/shard_map/all_gather | solution.py:71
  799.9 4.6 fusion.14
  804.5 0.0 reduce-scatter.8.cloned.1.call-start
  804.6 28.6 %all-gather.9.cloned.1.call-done = bf16[128,4096]{0,1:T(8,128)(2,1)} async-done(((bf16[128,512]{0,1:T(8,128)(2,1)}), bf16[128,4096]{0,1:T(8,128)(2,1)}) %all-gather.9.cloned.1.call-update) | async-done | bytes 1048592 | tf_op jit(solution)/shard_map/all_gather | solution.py:62
  833.1 4.4 convolution_convert_fusion
  837.7 239.7 %reduce-scatter.8.cloned.1.call-done = bf16[128,512]{1,0:T(8,128)(2,1)} async-done(((bf16[4096,512]{1,0:T(8,128)(2,1)}), bf16[128,512]{1,0:T(8,128)(2,1)}) %reduce-scatter.8.cloned.1.call-update) | async-done | bytes 131088 | tf_op jit(solution)/shard_map/reduce_scatter | solution.py:63
  1077.4 107.8 %all-gather.11.cloned.1.call-done = bf16[4096,512]{1,0:T(8,128)(2,1)} async-done(((bf16[128,512]{1,0:T(8,128)(2,1)}), bf16[4096,512]{1,0:T(8,128)(2,1)}) %all-gather.11.cloned.1.call-update) | async-done | bytes 4194320 | tf_op jit(solution)/shard_map/all_gather | solution.py:71
  1185.2 3.9 fusion.3
  1189.1 0.8 copy.28
  (39 shorter events, 0.4 us)
Async XLA Ops:
  6.5 2.9 copy-start.10
  6.5 333.3 %reduce-scatter.4.cloned.1.call-start = ((), (), s32[]{:S(2)}) async-start(), calls=%async_computation.3 | async-start | bytes 8650752 | tf_op jit(solution)/shard_map/reduce_scatter | solution.py:51
  30.6 6.3 copy-start.3
  36.9 2.9 copy-start.4
  36.9 2.9 copy-start.7
  39.8 1.6 copy-start.5
  39.8 1.8 copy-start.8
  41.7 1.5 copy-start.9
  43.2 2.2 copy-start.1
  43.2 3.5 copy-start.11
  70.6 377.5 %all-gather.5.cloned.1.call-start = ((), (), s32[]{:S(2)}) async-start(), calls=%async_computation.4 | async-start | bytes 1179648 | tf_op jit(solution)/shard_map/all_gather | solution.py:62
  417.0 276.2 %reduce-scatter.6.cloned.1.call-start = ((), (), s32[]{:S(2)}) async-start(), calls=%async_computation.5 | async-start | bytes 4325376 | tf_op jit(solution)/shard_map/reduce_scatter | solution.py:63
  452.6 347.3 %copy-start.2 = (bf16[128,4096]{0,1:T(8,128)(2,1)S(1)}, bf16[128,4096]{0,1:T(8,128)(2,1)}, u32[]{:S(2)}) copy-start(bf16[128,4096]{0,1:T(8,128)(2,1)} %all-gather.5.cloned.1.call-done) | copy-start | bytes 3145732
  452.6 347.3 %copy-start.6 = (f32[128,512]{0,1:T(8,128)S(1)}, f32[128,512]{0,1:T(8,128)}, u32[]{:S(2)}) copy-start(f32[128,512]{0,1:T(8,128)} %reduce-scatter.4.cloned.1.call-done) | copy-start | bytes 786436
  452.6 347.3 %all-gather.7.cloned.1.call-start = ((), (), s32[]{:S(2)}) async-start(), calls=%async_computation.6 | async-start | bytes 4325376 | tf_op jit(solution)/shard_map/all_gather | solution.py:71
  693.2 140.0 %all-gather.9.cloned.1.call-start = ((), (), s32[]{:S(2)}) async-start(), calls=%async_computation.7 | async-start | bytes 1179648 | tf_op jit(solution)/shard_map/all_gather | solution.py:62
  804.5 272.8 %reduce-scatter.8.cloned.1.call-start = ((), (), s32[]{:S(2)}) async-start(), calls=%async_computation.8 | async-start | bytes 4325376 | tf_op jit(solution)/shard_map/reduce_scatter | solution.py:63
  837.6 347.6 %copy-start = (bf16[128,4096]{0,1:T(8,128)(2,1)S(1)}, bf16[128,4096]{0,1:T(8,128)(2,1)}, u32[]{:S(2)}) copy-start(bf16[128,4096]{0,1:T(8,128)(2,1)} %all-gather.9.cloned.1.call-done) | copy-start | bytes 3145732
  837.6 347.5 %all-gather.11.cloned.1.call-start = ((), (), s32[]{:S(2)}) async-start(), calls=%async_computation.9 | async-start | bytes 4325376 | tf_op jit(solution)/shard_map/all_gather | solution.py:71
Sparse Core Ops, SparseCore 0:
  70.7 269.1 reduce-scatter.3
  417.1 31.0 all-gather.4
  452.7 240.3 reduce-scatter.5
  696.5 103.3 all-gather.6
  804.6 28.4 all-gather.8
  837.7 239.5 reduce-scatter.7
  1080.9 104.2 all-gather.10
where the time goes:
time: 1200 us
  waiting for transfers between devices  1020 us (85%)
  blocking collectives  86.8 us (7%)
  matrix products  35 us (3%)
  local copies, waits for them, and re-layouts  21.9 us (2%)
  other arithmetic  15.8 us (1%)
  between operations  14.4 us (1%)
    reduce_scatter x2, waiting for transfers between devices, shards(): lax.psum_scatter(contract_rows(row_panel, half_iter).astype(jnp.bfloat16)...  480 us
    reduce_scatter x1, waiting for transfers between devices, shards(): lax.psum_scatter(contract_rows(embeddings, weighted), 'dp', scatter_dimen...  268 us
    all_gather x2, waiting for transfers between devices, shards(): lax.all_gather(gram_block, 'dp', axis=0, tiled=True)  214 us
    psum x1, blocking collectives, shards(): frob_total = lax.psum(jnp.sum(cross_block * cross_block), ('dp', 'col'))  73.1 us
    all_gather x2, waiting for transfers between devices, shards(): row_panel = lax.all_gather(half_iter, 'col', axis=1, tiled=True)  59.5 us
  transfers between devices with their start and end apart: 7, of which 7 were waited for; matrix products, arithmetic and copies ran while one was open for 0% of the time, Pallas kernels for 0%

commit v1 on v0

--- a/solution.py
+++ b/solution.py
@@ -68,7 +68,9 @@
         )
         product = jnp.dot(
             row_panel,
-            lax.all_gather(gram_block, "dp", axis=0, tiled=True),
+            jnp.concatenate(
+                lax.all_to_all(jnp.stack([gram_block] * lax.axis_size("dp")), "dp", 0, 0), axis=0
+            ),
             preferred_element_type=jnp.float32,
         )
         iterate = 1.5 * iterate - 0.5 * product

time: 1200 us -> 1140 us (0.950); the launches traced: 1200 us -> 1120 us
  waiting for transfers between devices: 1020 us -> 814 us
  blocking collectives: 86.8 us -> 223 us
    all_gather x2 -> x0, waiting for transfers between devices: 214 us -> none  [shards(): lax.all_gather(gram_block, 'dp', axis=0, tiled=True)]
    all_to_all x0 -> x2, blocking collectives: none -> 131 us  [shards(): lax.all_to_all(jnp.stack([gram_block] * lax.axis_size('dp')), 'dp', 0, 0)]
  transfers between devices with their start and end apart: 7 -> 5, of which waited for: 7 -> 5; matrix products, arithmetic and copies ran while one was open for 0% -> 0% of each run, Pallas kernels for 0% -> 0%
where the time goes in v1:
time: 1140 us; the launch traced here: 1120 us
  waiting for transfers between devices  814 us (71%)
  blocking collectives  223 us (20%)
  matrix products  30.7 us (3%)
  local copies, waits for them, and re-layouts  24.5 us (2%)
  other arithmetic  15.8 us (1%)
  between operations  14.1 us (1%)
    reduce_scatter x2, waiting for transfers between devices, shards(): lax.psum_scatter(contract_rows(row_panel, half_iter).astype(jnp.bfloat16)...  490 us
    reduce_scatter x1, waiting for transfers between devices, shards(): lax.psum_scatter(contract_rows(embeddings, weighted), 'dp', scatter_dimen...  261 us
    all_to_all x2, blocking collectives, shards(): lax.all_to_all(jnp.stack([gram_block] * lax.axis_size('dp')), 'dp', 0, 0)  131 us
    psum x1, blocking collectives, shards(): frob_total = lax.psum(jnp.sum(cross_block * cross_block), ('dp', 'col'))  77.5 us
    all_gather x2, waiting for transfers between devices, shards(): row_panel = lax.all_gather(half_iter, 'col', axis=1, tiled=True)  63.5 us
  transfers between devices with their start and end apart: 5, of which 5 were waited for; matrix products, arithmetic and copies ran while one was open for 0% of the time, Pallas kernels for 0%

profile of v1, /device:TPU:32, one launch (start us, length us, event | category | flops | bytes accessed | tf_op | source)
XLA Modules:
  0.0 1122.4 jit_solution(6493240587937093548)
XLA Ops:
  6.5 1.0 fusion.12
  7.6 0.4 multiply_bitcast_fusion.3
  8.0 1.4 copy.37
  9.4 0.1 copy.21
  9.6 3.0 iota_compare_fusion.1
  12.6 2.9 copy.36
  15.5 1.4 copy.35
  16.9 0.1 copy.19
  17.1 3.0 iota_compare_fusion.2
  20.1 2.9 copy.34
  23.0 1.5 copy.33
  24.5 0.1 copy.17
  24.6 3.0 iota_compare_fusion.3
  27.6 2.9 copy.32
  30.5 1.4 copy.39
  31.9 0.1 copy.23
  32.0 3.2 iota_compare_fusion
  35.2 1.6 copy.38
  36.9 2.9 convolution_convert_fusion.3
  39.8 1.5 convolution_convert_fusion.4
  41.4 0.3 copy-done.8
  41.6 1.5 convolution_convert_fusion.5
  43.2 1.5 convolution_convert_fusion.2
  44.7 0.6 copy-done.1
  45.4 1.3 copy-done.11
  46.6 2.4 fusion.1
  49.0 13.7 %psum.14 = f32[512]{0:T(512)S(1)} all-reduce(f32[512]{0:T(512)S(1)} %fusion.1), channel_id=1, replica_groups=mesh['dp'=32,'col'=8] {'col'}, use_global_device_ids=true, to_apply=%region_1.0 | all-reduce | flops 512 | bytes 4096 | tf_op jit(solution)/shard_map/psum | solution.py:48
  62.7 7.8 convolution_bitcast_fusion
  70.6 0.9 constant_dynamic-slice_fusion
  71.5 0.1 copy.31
  71.6 260.9 %reduce-scatter.4.cloned.1.call-done = f32[128,512]{0,1:T(8,128)} async-done(((f32[4096,512]{0,1:T(8,128)}), f32[128,512]{0,1:T(8,128)}) %reduce-scatter.4.cloned.1.call-update) | async-done | bytes 262160 | tf_op jit(solution)/shard_map/reduce_scatter | solution.py:51
  332.5 1.6 multiply_reduce_fusion
  334.2 77.5 %psum.15 = f32[]{:T(128)} all-reduce(f32[]{:T(128)} %multiply_reduce_fusion), channel_id=1, replica_groups=mesh['dp'=32,'col'=8] {'dp','col'}, use_global_device_ids=true, to_apply=%region_4.0 | all-reduce | flops 1 | bytes 8 | tf_op jit(solution)/shard_map/psum | solution.py:57
  412.4 1.7 fusion.9
  414.1 0.3 reduce-scatter.6.cloned.1.call-start
  414.3 31.8 %all-gather.3.cloned.1.call-done = bf16[128,4096]{0,1:T(8,128)(2,1)} async-done(((bf16[128,512]{0,1:T(8,128)(2,1)}), bf16[128,4096]{0,1:T(8,128)(2,1)}) %all-gather.3.cloned.1.call-update) | async-done | bytes 1048592 | tf_op jit(solution)/shard_map/all_gather | solution.py:62
  446.2 4.4 convolution_convert_fusion.1
  450.7 245.5 %reduce-scatter.6.cloned.1.call-done = bf16[128,512]{1,0:T(8,128)(2,1)} async-done(((bf16[4096,512]{1,0:T(8,128)(2,1)}), bf16[128,512]{1,0:T(8,128)(2,1)}) %reduce-scatter.6.cloned.1.call-update) | async-done | bytes 131088 | tf_op jit(solution)/shard_map/reduce_scatter | solution.py:63
  696.2 1.4 stack.4
  697.6 74.6 %all_to_all.10 = bf16[32,128,512]{2,1,0:T(8,128)(2,1)S(1)} all-to-all(bf16[32,128,512]{2,1,0:T(8,128)(2,1)S(1)} %stack.4), channel_id=1, replica_groups=mesh['dp'=32,'col'=8] {'dp'}, dimensions={0} | all-to-all | bytes 8388608 | tf_op jit(solution)/shard_map/all_to_all | solution.py:72
  772.2 2.4 fusion.14
  774.7 31.7 %all-gather.5.cloned.1.call-done = bf16[128,4096]{0,1:T(8,128)(2,1)} async-done(((bf16[128,512]{0,1:T(8,128)(2,1)}), bf16[128,4096]{0,1:T(8,128)(2,1)}) %all-gather.5.cloned.1.call-update) | async-done | bytes 1048592 | tf_op jit(solution)/shard_map/all_gather | solution.py:62
  806.4 4.4 convolution_convert_fusion
  810.8 244.3 %reduce-scatter.8.cloned.1.call-done = bf16[128,512]{1,0:T(8,128)(2,1)} async-done(((bf16[4096,512]{1,0:T(8,128)(2,1)}), bf16[128,512]{1,0:T(8,128)(2,1)}) %reduce-scatter.8.cloned.1.call-update) | async-done | bytes 131088 | tf_op jit(solution)/shard_map/reduce_scatter | solution.py:63
  1055.1 1.4 stack.5
  1056.5 56.7 %all_to_all.11 = bf16[32,128,512]{2,1,0:T(8,128)(2,1)S(1)} all-to-all(bf16[32,128,512]{2,1,0:T(8,128)(2,1)S(1)} %stack.5), channel_id=1, replica_groups=mesh['dp'=32,'col'=8] {'dp'}, dimensions={0} | all-to-all | bytes 8388608 | tf_op jit(solution)/shard_map/all_to_all | solution.py:72
  1113.2 1.8 fusion.3
  1115.0 0.8 copy.28
  (37 shorter events, 0.4 us)
Async XLA Ops:
  6.5 2.9 copy-start.10
  6.5 326.0 %reduce-scatter.4.cloned.1.call-start = ((), (), s32[]{:S(2)}) async-start(), calls=%async_computation.5 | async-start | bytes 8650752 | tf_op jit(solution)/shard_map/reduce_scatter | solution.py:51
  30.5 6.3 copy-start.3
  36.8 2.9 copy-start.4
  36.8 2.9 copy-start.7
  39.8 1.6 copy-start.5
  39.8 1.8 copy-start.8
  41.6 1.5 copy-start.9
  43.2 2.2 copy-start.1
  43.2 3.5 copy-start.11
  70.5 375.6 %all-gather.3.cloned.1.call-start = ((), (), s32[]{:S(2)}) async-start(), calls=%async_computation.6 | async-start | bytes 1179648 | tf_op jit(solution)/shard_map/all_gather | solution.py:62
  414.1 282.1 %reduce-scatter.6.cloned.1.call-start = ((), (), s32[]{:S(2)}) async-start(), calls=%async_computation.7 | async-start | bytes 4325376 | tf_op jit(solution)/shard_map/reduce_scatter | solution.py:63
  450.6 355.8 %all-gather.5.cloned.1.call-start = ((), (), s32[]{:S(2)}) async-start(), calls=%async_computation.8 | async-start | bytes 1179648 | tf_op jit(solution)/shard_map/all_gather | solution.py:62
  697.6 74.6 %copy-start.2 = (bf16[128,4096]{0,1:T(8,128)(2,1)S(1)}, bf16[128,4096]{0,1:T(8,128)(2,1)}, u32[]{:S(2)}) copy-start(bf16[128,4096]{0,1:T(8,128)(2,1)} %all-gather.3.cloned.1.call-done) | copy-start | bytes 3145732
  697.6 74.6 %copy-start.6 = (f32[128,512]{0,1:T(8,128)S(1)}, f32[128,512]{0,1:T(8,128)}, u32[]{:S(2)}) copy-start(f32[128,512]{0,1:T(8,128)} %reduce-scatter.4.cloned.1.call-done) | copy-start | bytes 786436
  774.6 280.5 %reduce-scatter.8.cloned.1.call-start = ((), (), s32[]{:S(2)}) async-start(), calls=%async_computation.9 | async-start | bytes 4325376 | tf_op jit(solution)/shard_map/reduce_scatter | solution.py:63
  1056.5 56.7 %copy-start = (bf16[128,4096]{0,1:T(8,128)(2,1)S(1)}, bf16[128,4096]{0,1:T(8,128)(2,1)}, u32[]{:S(2)}) copy-start(bf16[128,4096]{0,1:T(8,128)(2,1)} %all-gather.5.cloned.1.call-done) | copy-start | bytes 3145732
Sparse Core Ops, SparseCore 0:
  70.6 261.8 reduce-scatter.3
  414.2 31.9 all-gather.2
  450.7 245.4 reduce-scatter.5
  774.7 31.5 all-gather.4
  811.0 244.1 reduce-scatter.7
